TPU v7x, 128 devices: a whole 4x4x4 slice. The times are simulated.
128 devices in a mesh: pos: 16 (over x, y), obj: 8 (over z, core).
Axes of the slice: x: 4, y: 4, z: 4, core: 2. Of those that a mesh axis runs over, the one named last changes fastest.
Arguments:
- object_field: float32 [2, 4096, 6144], P(None, 'obj', 'pos'), may hold values from -5 to 5
- probe: float32 [2, 256, 256], replicated, may hold values from -5 to 5
- amplitude: bfloat16 [2048, 256, 256], P(('pos', 'obj')), may hold values from 0.19921875 to 3
- row_offset: int32 [2048], P(('pos', 'obj')), may hold values from 0 to 256
- col_offset: int32 [2048], P(('pos', 'obj')), may hold values from 0 to 128
- owner: int32 [2048], P(('pos', 'obj')), may hold values from 0 to 15, as said below
Outputs:
- new_object: float32 [2, 4096, 6144], P(None, 'obj', 'pos')
- new_probe: float32 [2, 256, 256], replicated
Inputs may be any that keep to these rules, and one draw needn't show every extreme that they name: Among the 16 positions of one device no owner is named more than 2 times; in each row band one owner is named exactly 2 times by every device.
All inputs are finite; a program needn't handle non-finite values.
Results may differ from a plain program's by a relative error of at most 0.005.
The roundings to bfloat16 on the way count: a program that leaves them out, or rounds other values in their place, can miss the bound.
Values may be sent and summed in bfloat16 or wider, within the bound.
A program may use at most 128 MiB of HBM per device.

v0:
```python
import math
import jax
import jax.numpy as jnp
from jax import lax
from jax.sharding import PartitionSpec as P


def padded_2(block, sides, width):
    for axis, dim in sides:
        count = lax.axis_size(axis)
        forward = [(i, i + 1) for i in range(count - 1)]
        forward.append((count - 1, 0))
        backward = [(target, source) for source, target in forward]
        low = lax.ppermute(
            lax.slice_in_dim(block, block.shape[dim] - width, None, axis=dim), axis, forward
        )
        high = lax.ppermute(lax.slice_in_dim(block, 0, width, axis=dim), axis, backward)
        block = jnp.concatenate([low, block, high], axis=dim)
    return block


def dft_tables(size):
    index = jnp.arange(size, dtype=jnp.int32)
    product = index[:, None] * index[None, :] % size
    angle = product.astype(jnp.float32) * (2.0 * math.pi / size)
    scale = 1.0 / math.sqrt(size)
    real_part = (jnp.cos(angle) * scale).astype(jnp.bfloat16)
    imag_part = (-jnp.sin(angle) * scale).astype(jnp.bfloat16)
    return (real_part, imag_part)


def left_apply(mat_re, mat_im, val_re, val_im):

    def product(matrix, values):
        return jnp.einsum("jk,bkl->bjl", matrix, values, preferred_element_type=jnp.float32)

    return (
        product(mat_re, val_re) - product(mat_im, val_im),
        product(mat_re, val_im) + product(mat_im, val_re),
    )


def right_apply(val_re, val_im, mat_re, mat_im):

    def product(values, matrix):
        return jnp.einsum("bjk,kl->bjl", values, matrix, preferred_element_type=jnp.float32)

    return (
        product(val_re, mat_re) - product(val_im, mat_im),
        product(val_re, mat_im) + product(val_im, mat_re),
    )


def position_terms(patches, amps, validity, probe, tables):
    four_re, four_im, conj_im = tables
    patch_re = patches[:, 0].astype(jnp.float32)
    patch_im = patches[:, 1].astype(jnp.float32)
    probe_re = probe[0]
    probe_im = probe[1]
    psi_re = (probe_re * patch_re - probe_im * patch_im).astype(jnp.bfloat16)
    psi_im = (probe_re * patch_im + probe_im * patch_re).astype(jnp.bfloat16)
    left_re, left_im = left_apply(four_re, four_im, psi_re, psi_im)
    wave_re, wave_im = right_apply(
        left_re.astype(jnp.bfloat16), left_im.astype(jnp.bfloat16), four_re, four_im
    )
    magnitude = jnp.sqrt(wave_re * wave_re + wave_im * wave_im)
    factor = 1.0 - amps.astype(jnp.float32) / jnp.maximum(magnitude, 0.5)
    diff_re = (wave_re * factor).astype(jnp.bfloat16)
    diff_im = (wave_im * factor).astype(jnp.bfloat16)
    back_re, back_im = left_apply(four_re, conj_im, diff_re, diff_im)
    chi_re, chi_im = right_apply(
        back_re.astype(jnp.bfloat16), back_im.astype(jnp.bfloat16), four_re, conj_im
    )
    chi_re = chi_re * validity[:, None, None]
    chi_im = chi_im * validity[:, None, None]
    grad_re = (probe_re * chi_re + probe_im * chi_im).astype(jnp.bfloat16)
    grad_im = (probe_re * chi_im - probe_im * chi_re).astype(jnp.bfloat16)
    term_re = jnp.sum(patch_re * chi_re + patch_im * chi_im, axis=0)
    term_im = jnp.sum(patch_re * chi_im - patch_im * chi_re, axis=0)
    return (jnp.stack([grad_re, grad_im], axis=1), jnp.stack([term_re, term_im]))


def run_terms(patches, amps, validity, probe, tables):
    count = patches.shape[0]
    size = patches.shape[2]
    batch_size = math.gcd(count, 8)
    groups = count // batch_size
    grouped = (
        patches.reshape(groups, batch_size, 2, size, size),
        amps.reshape(groups, batch_size, size, size),
        validity.reshape(groups, batch_size),
    )
    grads, terms = lax.map(
        lambda items: position_terms(items[0], items[1], items[2], probe, tables), grouped
    )
    return (grads.reshape(count, 2, size, size), jnp.sum(terms, axis=0))


def extract(tile, corners, size):
    zero = jnp.zeros((), jnp.int32)
    windows = jax.vmap(lambda row, col: lax.dynamic_slice(tile, (zero, row, col), (2, size, size)))(
        corners[:, 0], corners[:, 1]
    )
    return windows.astype(jnp.bfloat16)


def add_scaled(start_value, grads, corners, size):
    zero = jnp.zeros((), jnp.int32)

    def add_one(item, acc):
        corner = (zero, corners[item, 0], corners[item, 1])
        window = lax.dynamic_slice(acc, corner, (2, size, size))
        return lax.dynamic_update_slice(
            acc, window - 0.25 * grads[item].astype(jnp.float32), corner
        )

    return lax.fori_loop(0, grads.shape[0], add_one, start_value)


def shards(object_field, probe, amplitude, row_offset, col_offset, owner):
    n_pos = lax.axis_size("pos")
    n_obj = lax.axis_size("obj")
    pos_dev = amplitude.shape[0]
    size = amplitude.shape[1]
    capacity = max(2, pos_dev // n_pos + 1)
    slots = n_pos * capacity
    padded = padded_2(object_field.astype(jnp.bfloat16), (("pos", 2), ("obj", 1)), 1).astype(
        object_field.dtype
    )
    smooth = 4.0 * object_field - padded[:, :-2, 1:-1] - padded[:, 2:, 1:-1]
    smooth = smooth - padded[:, 1:-1, :-2] - padded[:, 1:-1, 2:]
    four_re, four_im = dft_tables(size)
    tables = (four_re, four_im, -four_im)
    onehot = (owner[:, None] == jnp.arange(n_pos, dtype=jnp.int32)[None, :]).astype(jnp.int32)
    earlier = jnp.cumsum(onehot, axis=0) - onehot
    ranking = jnp.sum(earlier * onehot, axis=1)
    target = owner * capacity + ranking
    matching = (target[:, None] == jnp.arange(slots, dtype=jnp.int32)[None, :]).astype(jnp.int32)
    source = jnp.sum(matching * jnp.arange(pos_dev, dtype=jnp.int32)[:, None], axis=0)
    filled = jnp.sum(matching, axis=0) > 0
    listing = jnp.stack([row_offset, col_offset, jnp.ones_like(row_offset)], axis=1)
    slot_info = jnp.where(filled[:, None], listing[source], 0).reshape(n_pos, capacity, 3)
    received = lax.all_to_all(slot_info, "pos", split_axis=0, concat_axis=0, tiled=True)
    items = received.shape[1]
    windows = extract(object_field, received.reshape(-1, 3), size)
    windows = windows.reshape(n_pos, items, 2, size, size)
    fetched = lax.all_to_all(windows, "pos", split_axis=0, concat_axis=0, tiled=True)
    mine = fetched.reshape(slots, 2, size, size)[target]
    grads, probe_part = run_terms(mine, amplitude, jnp.ones((pos_dev,), jnp.float32), probe, tables)
    grad_slots = jnp.where(filled[:, None, None, None], grads[source], jnp.zeros((), jnp.bfloat16))
    incoming = lax.all_to_all(
        grad_slots.reshape(n_pos, capacity, 2, size, size),
        "pos",
        split_axis=0,
        concat_axis=0,
        tiled=True,
    )
    incoming = incoming.reshape(slots, 2, size, size)
    corners = received.reshape(slots, 3)
    base = object_field - 0.125 * smooth
    new_object = add_scaled(base, incoming, corners, size)
    probe_grad = lax.psum(probe_part, ("pos", "obj"))
    n_total = pos_dev * n_pos * n_obj
    new_probe = probe - probe_grad * (1.0 / math.sqrt(n_total))
    return (new_object, new_probe)


def solution(mesh):
    placed = (
        P(None, "obj", "pos"),
        P(),
        P(("pos", "obj"), None, None),
        P(("pos", "obj")),
        P(("pos", "obj")),
        P(("pos", "obj")),
    )
    return jax.shard_map(
        shards, mesh=mesh, in_specs=placed, out_specs=(P(None, "obj", "pos"), P()), check_vma=False
    )
```

profile of v0, /device:TPU:15, one launch (start us, length us, event | category | flops | bytes accessed | tf_op | source)
XLA Modules:
  0.0 1008.5 jit_solution(17226852778361089383)
XLA Ops:
  12.1 6.8 all-to-all-start
  20.4 2.3 all-to-all-done
  22.9 89.1 %while.29 = (s32[]{:T(128)}, bf16[2,512,384]{2,1,0:T(8,128)(2,1)S(1)}, s32[32,3]{0,1:T(4,128)S(1)}, bf16[32,2,256,256]{3,2,1,0:T(8,128)(2,1)}, s32[]{:T(128)}) while((s32[]{:T(128)}, bf16[2,512,384]{2,1,0:T(8,128)(2,1)S(1)}, s32[32,3]{0,1:T(4,128)S(1)}, bf16[32,2,256,256]{3,2,1,0:T(8,128)(2,1)}, s32[]{:T(128)}) %tuple.89), condition=%wide.while_cond, body=%wide.while_body.sunk | while | flops 2 | bytes 525929 | solution.py:101
  23.5 2.2 bitcast_dynamic-update-slice_fusion.2
  26.3 2.2 bitcast_dynamic-update-slice_fusion.2
  29.1 2.2 bitcast_dynamic-update-slice_fusion.2
  43.0 2.2 bitcast_dynamic-update-slice_fusion.2
  45.8 2.2 bitcast_dynamic-update-slice_fusion.2
  48.6 2.2 bitcast_dynamic-update-slice_fusion.2
  70.9 2.2 bitcast_dynamic-update-slice_fusion.2
  73.6 2.2 bitcast_dynamic-update-slice_fusion.2
  82.0 2.2 bitcast_dynamic-update-slice_fusion.2
  90.3 2.2 bitcast_dynamic-update-slice_fusion.2
  101.5 2.2 bitcast_dynamic-update-slice_fusion.2
  104.3 2.2 bitcast_dynamic-update-slice_fusion.2
  112.9 7.2 all-to-all-start.1
  120.1 130.6 %all-to-all-done.1 = bf16[16,2,2,256,256]{4,3,2,1,0:T(8,128)(2,1)} async-done(((bf16[16,2,2,256,256]{4,3,2,1,0:T(8,128)(2,1)}), bf16[16,2,2,256,256]{4,3,2,1,0:T(8,128)(2,1)}, u32[]{:S(2)}, u32[]{:S(2)}) %all-to-all-start.1) | async-done | bytes 8388640 | tf_op jit(solution)/shard_map/all_to_all | solution.py:147
  250.7 6.2 gather_fusion.1
  256.9 60.2 %while.30 = (s32[]{:T(128)}, bf16[2,8,2,256,256]{4,3,2,1,0:T(8,128)(2,1)}, f32[2,2,256,256]{3,2,1,0:T(8,128)S(1)}, f32[2,256,256]{2,1,0:T(8,128)S(1)}, bf16[2,8,...) while((s32[]{:T(128)}, ...), condition=%wide.region_7.8_spmd.clone.clone, body=%wide.region_4.7_spmd.clone.clone.sunk | while | flops 4348182528 | bytes 96470128 | solution.py:93
  269.8 2.8 multiply_convert_fusion.9
  282.5 3.0 fusion.253
  299.9 2.8 multiply_convert_fusion.9
  312.5 3.0 fusion.253
  317.1 7.5 gather_fusion.2
  324.6 7.2 broadcast_select_fusion
  331.8 9.4 all-to-all-start.2
  342.9 91.4 %collective-permute-done = bf16[2,512,1]{2,1,0:T(8,128)(2,1)S(1)} collective-permute-done((bf16[2,512,1]{2,1,0:T(8,128)(2,1)S(1)}, bf16[2,512,1]{2,1,0:T(8,128)(2,1)S(1)}, u32[]{:S(2)}, u32[]{:S(2)}) %collective-permute-start) | collective-permute-done | bytes 2080 | tf_op jit(solution)/shard_map/ppermute | solution.py:14
  435.7 11.3 %collective-permute-start.2 = (bf16[2,1,386]{2,1,0:T(2,128)(2,1)S(1)}, bf16[2,1,386]{2,1,0:T(2,128)(2,1)S(1)}, u32[]{:S(2)}, u32[]{:S(2)}) collective-permute-start(bf16[2,1,386]{2,1,0:T(2,128)(2,1)S(1)} %get-tuple-element.299), channel_id=1, source_target_pairs={{0,1},{1,2},{2,3},{3,4},{4,5},{5,6},{6,7},{7,0},{8,9},{9,10},{10,1... | collective-permute-start | bytes 4640 | tf_op jit(solution)/shard_map/ppermute | solution.py:14
  447.8 2.3 collective-permute-done.3
  454.1 3.9 fusion.143
  458.0 151.4 %all-reduce.2.cloned.1.call-done = f32[2,256,256]{2,1,0:T(8,128)} async-done(((f32[2,256,256]{2,1,0:T(8,128)}), f32[2,256,256]{2,1,0:T(8,128)}) %all-reduce.2.cloned.1.call-update) | async-done | bytes 524304 | tf_op jit(solution)/shard_map/psum | solution.py:162
  611.3 390.4 %while.28 = (s32[]{:T(128)}, f32[2,512,384]{2,1,0:T(8,128)}, s32[32,3]{0,1:T(4,128)S(1)}, bf16[32,2,256,256]{3,2,1,0:T(8,128)(2,1)}, s32[]{:T(128)}, /*index=5*/s32[]{:T(128)}, s32[]{:T(128)}, s32[]{:T(128)}) while((s32[]{:T(128)}, f32[2,512,384]{2,1,0:T(8,128)}, s32[32,3]{0,1:T(4,128)S(1)}, bf16[32,2,256,256]{3,2,1,0:T(8,128)(2,1)}, ...), condition=%wide.region_9.10_spmd, body=%wide.region_8.9_spmd.sunk | while | flops 393224 | bytes 2359485 | solution.py:117
  617.2 6.4 dynamic_update_slice.24
  629.4 6.1 dynamic_update_slice.24
  641.4 6.5 dynamic_update_slice.24
  653.7 6.0 dynamic_update_slice.24
  665.7 6.5 dynamic_update_slice.24
  678.0 6.5 dynamic_update_slice.24
  690.4 6.5 dynamic_update_slice.24
  702.7 6.5 dynamic_update_slice.24
  715.1 6.5 dynamic_update_slice.24
  727.5 6.4 dynamic_update_slice.24
  739.8 6.5 dynamic_update_slice.24
  752.1 6.3 dynamic_update_slice.24
  764.3 6.3 dynamic_update_slice.24
  776.5 6.4 dynamic_update_slice.24
  788.7 6.4 dynamic_update_slice.24
  801.0 6.5 dynamic_update_slice.24
  813.4 6.0 dynamic_update_slice.24
  825.3 6.4 dynamic_update_slice.24
  837.5 6.5 dynamic_update_slice.24
  849.9 5.9 dynamic_update_slice.24
  861.7 6.2 dynamic_update_slice.24
  873.8 6.2 dynamic_update_slice.24
  885.8 6.4 dynamic_update_slice.24
  898.1 6.3 dynamic_update_slice.24
  910.3 6.5 dynamic_update_slice.24
  922.6 6.3 dynamic_update_slice.24
  934.8 6.1 dynamic_update_slice.24
  946.8 6.5 dynamic_update_slice.24
  959.1 6.0 dynamic_update_slice.24
  971.0 6.0 dynamic_update_slice.24
  982.9 6.5 dynamic_update_slice.24
  995.3 6.4 dynamic_update_slice.24
  (242 shorter events, 194.9 us)
Async XLA Ops:
  12.1 10.6 %all-to-all-start = ((s32[16,2,3]{2,1,0:T(2,128)}), s32[16,2,3]{2,1,0:T(2,128)S(1)}, u32[]{:S(2)}, u32[]{:S(2)}) async-start(s32[16,2,3]{2,1,0:T(2,128)} %copy.88), calls=%async_computation | async-start | bytes 32768 | tf_op jit(solution)/shard_map/all_to_all | solution.py:143
  22.8 89.2 %copy-start.6 = (s32[32,3]{0,1:T(4,128)}, s32[32,3]{0,1:T(4,128)S(1)}, u32[]{:S(2)}) copy-start(s32[32,3]{0,1:T(4,128)S(1)} %copy.109) | copy-start | bytes 1156
  112.0 0.9 copy-start
  112.9 137.8 %all-to-all-start.1 = ((bf16[16,2,2,256,256]{4,3,2,1,0:T(8,128)(2,1)}), bf16[16,2,2,256,256]{4,3,2,1,0:T(8,128)(2,1)}, u32[]{:S(2)}, u32[]{:S(2)}) async-start(bf16[16,2,2,256,256]{4,3,2,1,0:T(8,128)(2,1)} %bitcast.241), calls=%async_computation.1 | async-start | bytes 16777216 | tf_op jit(solution)/shard_map/all_to_all | solution.py:147
  250.7 6.2 copy-start.2
  268.2 1.6 copy-start.8
  298.3 1.6 copy-start.8
  317.1 7.5 copy-start.3
  331.8 9.4 copy-start.1
  331.8 279.5 %all-to-all-start.2 = ((bf16[16,2,2,256,256]{4,3,2,1,0:T(8,128)(2,1)}), bf16[16,2,2,256,256]{4,3,2,1,0:T(8,128)(2,1)}, u32[]{:S(2)}, u32[]{:S(2)}) async-start(bf16[16,2,2,256,256]{4,3,2,1,0:T(8,128)(2,1)} %broadcast_select_fusion), calls=%async_computation.2 | async-start | bytes 16777216 | tf_op jit(solution)/shard_map/all_to_all | solution.py:151
  341.2 268.2 %all-reduce.2.cloned.1.call-start = ((), (), s32[]{:S(2)}) async-start(), calls=%async_computation.3 | async-start | bytes 1048576 | tf_op jit(solution)/shard_map/psum | solution.py:162
  341.4 92.9 %collective-permute-start = (bf16[2,512,1]{2,1,0:T(8,128)(2,1)S(1)}, bf16[2,512,1]{2,1,0:T(8,128)(2,1)S(1)}, u32[]{:S(2)}, u32[]{:S(2)}) collective-permute-start(bf16[2,512,1]{2,1,0:T(8,128)(2,1)S(1)} %get-tuple-element.301), channel_id=1, source_target_pairs={{0,8},{8,16},{16,24},{24,32},{32,40},{40,48},{48,56},{56,64},{64,7... | collective-permute-start | bytes 6152 | tf_op jit(solution)/shard_map/ppermute | solution.py:14
  342.6 91.7 %collective-permute-start.1 = (bf16[2,512,1]{2,1,0:T(8,128)(2,1)S(1)}, bf16[2,512,1]{2,1,0:T(8,128)(2,1)S(1)}, u32[]{:S(2)}, u32[]{:S(2)}) collective-permute-start(bf16[2,512,1]{2,1,0:T(8,128)(2,1)S(1)} %get-tuple-element.302), channel_id=1, source_target_pairs={{8,0},{16,8},{24,16},{32,24},{40,32},{48,40},{56,48},{64,56},{72,6... | collective-permute-start | bytes 6152 | tf_op jit(solution)/shard_map/ppermute | solution.py:17
  434.3 0.7 copy-start.4
  435.0 0.7 copy-start.5
  435.7 12.1 %collective-permute-start.2 = (bf16[2,1,386]{2,1,0:T(2,128)(2,1)S(1)}, bf16[2,1,386]{2,1,0:T(2,128)(2,1)S(1)}, u32[]{:S(2)}, u32[]{:S(2)}) collective-permute-start(bf16[2,1,386]{2,1,0:T(2,128)(2,1)S(1)} %get-tuple-element.299), channel_id=1, source_target_pairs={{0,1},{1,2},{2,3},{3,4},{4,5},{5,6},{6,7},{7,0},{8,9},{9,10},{10,1... | collective-permute-start | bytes 4640 | tf_op jit(solution)/shard_map/ppermute | solution.py:14
  447.1 3.0 collective-permute-start.3
  454.1 157.2 %copy-start.7 = (s32[32,3]{0,1:T(4,128)S(1)}, s32[32,3]{0,1:T(4,128)}, u32[]{:S(2)}) copy-start(s32[32,3]{0,1:T(4,128)} %copy-done.6) | copy-start | bytes 1156
Sparse Core Ops, SparseCore 0:
  454.2 155.1 all-reduce.1
where the time goes:
time: 1020 us; the launch traced here: 1010 us
  waiting for transfers between devices  379 us (37%)
  local copies, waits for them, and re-layouts  335 us (33%)
  loops' own time  122 us (12%)
  other arithmetic  70.1 us (7%)
  matrix products  53 us (5%)
  starting transfers between devices  36.3 us (4%)
  between operations  14.1 us (1%)
    dynamic_update_slice x32, local copies, waits for them, and re-layouts, add_one(): lax.dynamic_update_slice(acc, window - 0.25 * grads[item].astype(jnp.floa...  203 us
    psum x1, waiting for transfers between devices, shards(): probe_grad = lax.psum(probe_part, ('pos', 'obj'))  151 us
    all_to_all x1, waiting for transfers between devices, shards(): lax.all_to_all(windows, 'pos', split_axis=0, concat_axis=0, tiled=True)  131 us
    another operation x1, loops' own time, add_scaled(): return lax.fori_loop(0, grads.shape[0], add_one, start_value)  121 us
    ppermute x2, waiting for transfers between devices, padded_2(): lax.ppermute(lax.slice_in_dim(block, block.shape[dim] - width, None, axis...  92.1 us
    gather x96, local copies, waits for them, and re-layouts  89.1 us
    sub x32, other arithmetic, add_one(): window - 0.25 * grads[item].astype(jnp.float32)  45.3 us
    dot_general x16, matrix products, product(): jnp.einsum('bjk,kl->bjl', values, matrix, preferred_element_type=jnp.floa...  28.6 us
  transfers between devices with their start and end apart: 8, of which 6 were waited for; matrix products, arithmetic and copies ran while one was open for 1% of the time, Pallas kernels for 0%

commit v1 on v0

--- a/solution.py
+++ b/solution.py
@@ -159,7 +159,7 @@
     corners = received.reshape(slots, 3)
     base = object_field - 0.125 * smooth
     new_object = add_scaled(base, incoming, corners, size)
-    probe_grad = lax.psum(probe_part, ("pos", "obj"))
+    probe_grad = lax.psum(lax.psum(probe_part, "obj"), "pos")
     n_total = pos_dev * n_pos * n_obj
     new_probe = probe - probe_grad * (1.0 / math.sqrt(n_total))
     return (new_object, new_probe)

time: 1020 us -> 987 us (0.968)
  waiting for transfers between devices: 379 us -> 295 us
  local copies, waits for them, and re-layouts: 335 us -> 394 us
  other arithmetic: 70.1 us -> 58.7 us
    ppermute x2, waiting for transfers between devices: 92.1 us -> 23.9 us  [padded_2(): lax.ppermute(lax.slice_in_dim(block, block.shape[dim] - width, None, axis...]
    dynamic_update_slice x32, local copies, waits for them, and re-layouts: 203 us -> 263 us  [add_one(): lax.dynamic_update_slice(acc, window - 0.25 * grads[item].astype(jnp.floa...]
    psum x1 -> x2, waiting for transfers between devices: 151 us -> 136 us  [shards(): probe_grad = lax.psum(lax.psum(probe_part, 'obj'), 'pos')]
  transfers between devices with their start and end apart: 8 -> 9, of which waited for: 6 -> 7; matrix products, arithmetic and copies ran while one was open for 1% -> 1% of each run, Pallas kernels for 0% -> 0%
where the time goes in v1:
time: 987 us; the launch traced here: 977 us
  local copies, waits for them, and re-layouts  394 us (40%)
  waiting for transfers between devices  295 us (30%)
  loops' own time  126 us (13%)
  other arithmetic  58.7 us (6%)
  matrix products  53 us (5%)
  starting transfers between devices  36.2 us (4%)
  between operations  14.2 us (1%)
    dynamic_update_slice x32, local copies, waits for them, and re-layouts, add_one(): lax.dynamic_update_slice(acc, window - 0.25 * grads[item].astype(jnp.floa...  263 us
    psum x2, waiting for transfers between devices, shards(): probe_grad = lax.psum(lax.psum(probe_part, 'obj'), 'pos')  136 us
    all_to_all x1, waiting for transfers between devices, shards(): lax.all_to_all(windows, 'pos', split_axis=0, concat_axis=0, tiled=True)  131 us
    another operation x1, loops' own time, add_scaled(): return lax.fori_loop(0, grads.shape[0], add_one, start_value)  126 us
    gather x96, local copies, waits for them, and re-layouts  88.2 us
    sub x32, other arithmetic, add_one(): window - 0.25 * grads[item].astype(jnp.float32)  37.3 us
    dot_general x16, matrix products, product(): jnp.einsum('bjk,kl->bjl', values, matrix, preferred_element_type=jnp.floa...  28.6 us
    dot_general x16, matrix products, product(): jnp.einsum('jk,bkl->bjl', matrix, values, preferred_element_type=jnp.floa...  24.5 us
  transfers between devices with their start and end apart: 9, of which 7 were waited for; matrix products, arithmetic and copies ran while one was open for 1% of the time, Pallas kernels for 0%

profile of v1, /device:TPU:15, one launch (start us, length us, event | category | flops | bytes accessed | tf_op | source)
XLA Modules:
  0.0 977.3 jit_solution(16186949601398293141)
XLA Ops:
  12.1 6.8 all-to-all-start
  20.4 2.3 all-to-all-done
  22.9 88.3 %while.29 = (s32[]{:T(128)}, bf16[2,512,384]{2,1,0:T(8,128)(2,1)S(1)}, s32[32,3]{0,1:T(4,128)S(1)}, bf16[32,2,256,256]{3,2,1,0:T(8,128)(2,1)}, s32[]{:T(128)}) while((s32[]{:T(128)}, bf16[2,512,384]{2,1,0:T(8,128)(2,1)S(1)}, s32[32,3]{0,1:T(4,128)S(1)}, bf16[32,2,256,256]{3,2,1,0:T(8,128)(2,1)}, s32[]{:T(128)}) %tuple.89), condition=%wide.while_cond, body=%wide.while_body.sunk | while | flops 2 | bytes 525929 | solution.py:101
  23.5 2.2 bitcast_dynamic-update-slice_fusion.2
  26.3 2.2 bitcast_dynamic-update-slice_fusion.2
  29.0 2.2 bitcast_dynamic-update-slice_fusion.2
  42.8 2.2 bitcast_dynamic-update-slice_fusion.2
  45.6 2.2 bitcast_dynamic-update-slice_fusion.2
  51.1 2.2 bitcast_dynamic-update-slice_fusion.2
  64.9 2.2 bitcast_dynamic-update-slice_fusion.2
  70.4 2.2 bitcast_dynamic-update-slice_fusion.2
  73.2 2.2 bitcast_dynamic-update-slice_fusion.2
  81.5 2.2 bitcast_dynamic-update-slice_fusion.2
  89.7 2.2 bitcast_dynamic-update-slice_fusion.2
  112.0 7.2 all-to-all-start.1
  119.3 130.6 %all-to-all-done.1 = bf16[16,2,2,256,256]{4,3,2,1,0:T(8,128)(2,1)} async-done(((bf16[16,2,2,256,256]{4,3,2,1,0:T(8,128)(2,1)}), bf16[16,2,2,256,256]{4,3,2,1,0:T(8,128)(2,1)}, u32[]{:S(2)}, u32[]{:S(2)}) %all-to-all-start.1) | async-done | bytes 8388640 | tf_op jit(solution)/shard_map/all_to_all | solution.py:147
  249.9 6.2 gather_fusion.1
  256.1 60.2 %while.30 = (s32[]{:T(128)}, bf16[2,8,2,256,256]{4,3,2,1,0:T(8,128)(2,1)}, f32[2,2,256,256]{3,2,1,0:T(8,128)S(1)}, f32[2,256,256]{2,1,0:T(8,128)S(1)}, bf16[2,8,...) while((s32[]{:T(128)}, ...), condition=%wide.region_7.8_spmd.clone.clone, body=%wide.region_4.7_spmd.clone.clone.sunk | while | flops 4348182528 | bytes 96470128 | solution.py:93
  269.0 2.8 multiply_convert_fusion.9
  281.6 3.0 fusion.253
  299.1 2.8 multiply_convert_fusion.9
  311.7 3.0 fusion.253
  316.3 7.1 gather_fusion.2
  323.4 7.2 broadcast_select_fusion
  330.6 9.3 all-to-all-start.2
  342.8 67.9 %all-reduce.3.cloned.1.call-done = f32[2,256,256]{2,1,0:T(8,128)} async-done(((f32[2,256,256]{2,1,0:T(8,128)}), f32[2,256,256]{2,1,0:T(8,128)}) %all-reduce.3.cloned.1.call-update) | async-done | bytes 524304 | tf_op jit(solution)/shard_map/psum | solution.py:162
  410.7 23.2 %collective-permute-done = bf16[2,512,1]{2,1,0:T(8,128)(2,1)S(1)} collective-permute-done((bf16[2,512,1]{2,1,0:T(8,128)(2,1)S(1)}, bf16[2,512,1]{2,1,0:T(8,128)(2,1)S(1)}, u32[]{:S(2)}, u32[]{:S(2)}) %collective-permute-start) | collective-permute-done | bytes 2080 | tf_op jit(solution)/shard_map/ppermute | solution.py:14
  434.0 11.3 %collective-permute-start.2 = (bf16[2,1,386]{2,1,0:T(2,128)(2,1)S(1)}, bf16[2,1,386]{2,1,0:T(2,128)(2,1)S(1)}, u32[]{:S(2)}, u32[]{:S(2)}) collective-permute-start(bf16[2,1,386]{2,1,0:T(2,128)(2,1)S(1)} %get-tuple-element.299), channel_id=1, source_target_pairs={{0,1},{1,2},{2,3},{3,4},{4,5},{5,6},{6,7},{7,0},{8,9},{9,10},{10,1... | collective-permute-start | bytes 4640 | tf_op jit(solution)/shard_map/ppermute | solution.py:14
  446.1 2.3 collective-permute-done.3
  449.2 2.8 fusion.143
  452.0 68.2 %all-reduce.5.cloned.1.call-done = f32[2,256,256]{2,1,0:T(8,128)} async-done(((f32[2,256,256]{2,1,0:T(8,128)}), f32[2,256,256]{2,1,0:T(8,128)}) %all-reduce.5.cloned.1.call-update) | async-done | bytes 524304 | tf_op jit(solution)/shard_map/psum | solution.py:162
  522.1 447.2 %while.28 = (s32[]{:T(128)}, f32[2,512,384]{2,1,0:T(8,128)S(1)}, s32[32,3]{0,1:T(4,128)S(1)}, bf16[32,2,256,256]{3,2,1,0:T(8,128)(2,1)}, s32[]{:T(128)}, /*index=5*/s32[]{:T(128)}, s32[]{:T(128)}, s32[]{:T(128)}) while((s32[]{:T(128)}, f32[2,512,384]{2,1,0:T(8,128)S(1)}, s32[32,3]{0,1:T(4,128)S(1)}, bf16[32,2,256,256]{3,2,1,0:T(8,128)(2,1)}, ...), condition=%wide.region_9.10_spmd, body=%wide.region_8.9_spmd.sunk | while | flops 393224 | bytes 2359485 | solution.py:117
  527.8 8.3 dynamic_update_slice.24
  541.9 7.4 dynamic_update_slice.24
  555.0 8.7 dynamic_update_slice.24
  569.5 7.3 dynamic_update_slice.24
  582.5 9.2 dynamic_update_slice.24
  597.4 8.8 dynamic_update_slice.24
  612.0 8.9 dynamic_update_slice.24
  626.6 9.2 dynamic_update_slice.24
  641.6 9.2 dynamic_update_slice.24
  656.6 8.4 dynamic_update_slice.24
  670.8 8.8 dynamic_update_slice.24
  685.4 8.0 dynamic_update_slice.24
  699.2 7.8 dynamic_update_slice.24
  712.7 8.1 dynamic_update_slice.24
  726.6 8.4 dynamic_update_slice.24
  740.8 9.2 dynamic_update_slice.24
  755.7 7.3 dynamic_update_slice.24
  768.7 8.1 dynamic_update_slice.24
  782.5 9.2 dynamic_update_slice.24
  797.5 7.0 dynamic_update_slice.24
  810.3 7.7 dynamic_update_slice.24
  823.7 7.5 dynamic_update_slice.24
  837.0 8.2 dynamic_update_slice.24
  850.9 7.9 dynamic_update_slice.24
  864.6 8.6 dynamic_update_slice.24
  878.9 8.0 dynamic_update_slice.24
  892.6 7.4 dynamic_update_slice.24
  905.8 8.8 dynamic_update_slice.24
  920.4 7.3 dynamic_update_slice.24
  933.4 7.3 dynamic_update_slice.24
  946.4 8.9 dynamic_update_slice.24
  961.1 8.2 dynamic_update_slice.24
  (241 shorter events, 186.0 us)
Async XLA Ops:
  12.1 10.6 %all-to-all-start = ((s32[16,2,3]{2,1,0:T(2,128)}), s32[16,2,3]{2,1,0:T(2,128)S(1)}, u32[]{:S(2)}, u32[]{:S(2)}) async-start(s32[16,2,3]{2,1,0:T(2,128)} %copy.88), calls=%async_computation | async-start | bytes 32768 | tf_op jit(solution)/shard_map/all_to_all | solution.py:143
  22.8 88.4 %copy-start.4 = (s32[32,3]{0,1:T(4,128)}, s32[32,3]{0,1:T(4,128)S(1)}, u32[]{:S(2)}) copy-start(s32[32,3]{0,1:T(4,128)S(1)} %copy.109) | copy-start | bytes 1156
  111.2 0.9 copy-start
  112.0 137.8 %all-to-all-start.1 = ((bf16[16,2,2,256,256]{4,3,2,1,0:T(8,128)(2,1)}), bf16[16,2,2,256,256]{4,3,2,1,0:T(8,128)(2,1)}, u32[]{:S(2)}, u32[]{:S(2)}) async-start(bf16[16,2,2,256,256]{4,3,2,1,0:T(8,128)(2,1)} %bitcast.241), calls=%async_computation.1 | async-start | bytes 16777216 | tf_op jit(solution)/shard_map/all_to_all | solution.py:147
  249.9 6.2 copy-start.2
  267.4 1.6 copy-start.6
  297.5 1.6 copy-start.6
  330.6 191.5 %all-to-all-start.2 = ((bf16[16,2,2,256,256]{4,3,2,1,0:T(8,128)(2,1)}), bf16[16,2,2,256,256]{4,3,2,1,0:T(8,128)(2,1)}, u32[]{:S(2)}, u32[]{:S(2)}) async-start(bf16[16,2,2,256,256]{4,3,2,1,0:T(8,128)(2,1)} %broadcast_select_fusion), calls=%async_computation.2 | async-start | bytes 16777216 | tf_op jit(solution)/shard_map/all_to_all | solution.py:151
  339.9 1.3 copy-start.1
  339.9 70.8 %all-reduce.3.cloned.1.call-start = ((), (), s32[]{:S(2)}) async-start(), calls=%async_computation.3 | async-start | bytes 1048576 | tf_op jit(solution)/shard_map/psum | solution.py:162
  340.8 179.4 %all-reduce.5.cloned.1.call-start = ((), (), s32[]{:S(2)}) async-start(), calls=%async_computation.4 | async-start | bytes 1048576 | tf_op jit(solution)/shard_map/psum | solution.py:162
  341.3 92.6 %collective-permute-start = (bf16[2,512,1]{2,1,0:T(8,128)(2,1)S(1)}, bf16[2,512,1]{2,1,0:T(8,128)(2,1)S(1)}, u32[]{:S(2)}, u32[]{:S(2)}) collective-permute-start(bf16[2,512,1]{2,1,0:T(8,128)(2,1)S(1)} %get-tuple-element.301), channel_id=1, source_target_pairs={{0,8},{8,16},{16,24},{24,32},{32,40},{40,48},{48,56},{56,64},{64,7... | collective-permute-start | bytes 6152 | tf_op jit(solution)/shard_map/ppermute | solution.py:14
  342.5 91.4 %collective-permute-start.1 = (bf16[2,512,1]{2,1,0:T(8,128)(2,1)S(1)}, bf16[2,512,1]{2,1,0:T(8,128)(2,1)S(1)}, u32[]{:S(2)}, u32[]{:S(2)}) collective-permute-start(bf16[2,512,1]{2,1,0:T(8,128)(2,1)S(1)} %get-tuple-element.302), channel_id=1, source_target_pairs={{8,0},{16,8},{24,16},{32,24},{40,32},{48,40},{56,48},{64,56},{72,6... | collective-permute-start | bytes 6152 | tf_op jit(solution)/shard_map/ppermute | solution.py:17
  434.0 12.1 %collective-permute-start.2 = (bf16[2,1,386]{2,1,0:T(2,128)(2,1)S(1)}, bf16[2,1,386]{2,1,0:T(2,128)(2,1)S(1)}, u32[]{:S(2)}, u32[]{:S(2)}) collective-permute-start(bf16[2,1,386]{2,1,0:T(2,128)(2,1)S(1)} %get-tuple-element.299), channel_id=1, source_target_pairs={{0,1},{1,2},{2,3},{3,4},{4,5},{5,6},{6,7},{7,0},{8,9},{9,10},{10,1... | collective-permute-start | bytes 4640 | tf_op jit(solution)/shard_map/ppermute | solution.py:14
  445.3 3.0 collective-permute-start.3
  449.2 72.9 %copy-start.5 = (s32[32,3]{0,1:T(4,128)S(1)}, s32[32,3]{0,1:T(4,128)}, u32[]{:S(2)}) copy-start(s32[32,3]{0,1:T(4,128)} %copy-done.4) | copy-start | bytes 1156
  969.3 1.1 copy-start.3
Sparse Core Ops, SparseCore 0:
  343.6 67.0 all-reduce.2
  414.2 105.9 all-reduce.4
